TPU v7x, 128 devices: a whole 4x4x4 slice. The times are simulated.
128 devices in a mesh: ctx: 16 (over x, z_hi, core), tp: 8 (over y, z_lo).
Axes of the slice: x: 4, y: 4, z: 4 (z_hi: 2, z_lo: 2; z = z_hi * 2 + z_lo), core: 2. Of those that a mesh axis runs over, the one named last changes fastest.
Arguments:
- query_proj: bfloat16 [6144, 4096], P('ctx', 'tp'), may hold values from -6 to 6
- key_proj: bfloat16 [6144, 4096], P('ctx', 'tp'), may hold values from -6 to 6
- value_proj: bfloat16 [6144, 4096], P('ctx', 'tp'), may hold values from -6 to 6
- saved_conv: bfloat16 [6144, 4096], P('ctx', 'tp'), may hold values from -6 to 6
- grad_out: bfloat16 [6144, 4096], P(('ctx', 'tp')), may hold values from -6 to 6
- filters: bfloat16 [256, 6144], P('tp'), may hold values from -0.109375 to 0.109375
- featurizer: float32 [3, 3, 4096], P(None, None, 'tp'), may hold values from -2 to 2
Outputs:
- grad_query: bfloat16 [6144, 4096], P('ctx', 'tp')
- grad_key: bfloat16 [6144, 4096], P('ctx', 'tp')
- grad_value: bfloat16 [6144, 4096], P('ctx', 'tp')
All inputs are finite; a program needn't handle non-finite values.
Results may differ from a plain program's by a relative error of at most 0.012.
Values may be sent and summed in bfloat16 or wider, within the bound.
A program may use at most 256 MiB of HBM per device.

v0:
```python
import jax
import jax.numpy as jnp
from jax import lax
from jax.sharding import PartitionSpec as P

GSIZE = 16
TAPS = 3


def shifted(array, axis, by):
    length = lax.axis_size(axis)
    pairs = [(i, i + by) for i in range(length) if 0 <= i + by < length]
    return lax.ppermute(array, axis, pairs)


def featurize(current, previous, kernel):
    amount = current.shape[0]
    joined = jnp.concatenate([previous, current], axis=0).astype(jnp.float32)
    total = kernel[0] * joined[TAPS - 1 : TAPS - 1 + amount]
    for offset in range(1, TAPS):
        total = total + kernel[offset] * joined[TAPS - 1 - offset : TAPS - 1 - offset + amount]
    return total


def spread(current, following, kernel):
    amount = current.shape[0]
    joined = jnp.concatenate([current, following], axis=0)
    total = kernel[0] * joined[0:amount]
    for offset in range(1, TAPS):
        total = total + kernel[offset] * joined[offset : offset + amount]
    return total


def toeplitz_tiles(window, tile_rows, width_k):
    groups = window.shape[0]
    padded = jnp.concatenate([window, jnp.zeros((groups, 1), window.dtype)], axis=1)
    tiled = jnp.tile(padded, (1, tile_rows))
    folded = tiled[:, : tile_rows * (width_k + tile_rows - 1)].reshape(
        groups, tile_rows, width_k + tile_rows - 1
    )
    return folded[:, :, tile_rows - 1 : tile_rows - 1 + width_k]


def cross_terms(source, src_start, dst_start, dst_rows, filt_pad, front_pad, tile_rows):
    groups = filt_pad.shape[0]
    src_rows = source.shape[0]
    src_tiles = -(-src_rows // tile_rows)
    dst_tiles = dst_rows // tile_rows
    width_k = (dst_tiles + src_tiles - 1) * tile_rows
    lag_first = src_start - dst_start - (dst_tiles - 1) * tile_rows - (tile_rows - 1)
    window = lax.dynamic_slice_in_dim(filt_pad, lag_first + front_pad, width_k + tile_rows - 1, 1)
    tiles = toeplitz_tiles(window, tile_rows, width_k)
    pieces = source.reshape(src_tiles, tile_rows, groups, GSIZE)
    result = jnp.zeros((dst_tiles, tile_rows, groups, GSIZE), jnp.float32)
    for diagonal in range(dst_tiles + src_tiles - 1):
        offset = diagonal - (dst_tiles - 1)
        lowest = max(0, -offset)
        highest = min(dst_tiles, src_tiles - offset)
        matrix = tiles[:, :, diagonal * tile_rows : (diagonal + 1) * tile_rows]
        product = jnp.einsum(
            "gij,ajgc->aigc",
            matrix,
            pieces[lowest + offset : highest + offset],
            preferred_element_type=jnp.float32,
        )
        result = result.at[lowest:highest].add(product)
    return result.reshape(dst_rows, groups * GSIZE)


def body(query_proj, key_proj, value_proj, saved_conv, grad_out, filters, featurizer):
    block_rows, channels = query_proj.shape
    tokens = filters.shape[1]
    tile_rows = min(128, block_rows)
    own_start = lax.axis_index("ctx") * block_rows
    front_pad = 2 * tokens
    filt_pad = jnp.pad(filters, ((0, 0), (front_pad, tokens + 2 * tile_rows)))
    upstream = lax.all_to_all(grad_out, "tp", split_axis=1, concat_axis=0, tiled=True)
    previous = shifted(
        (
            query_proj[block_rows - (TAPS - 1) :],
            key_proj[block_rows - (TAPS - 1) :],
            value_proj[block_rows - (TAPS - 1) :],
        ),
        "ctx",
        1,
    )
    query_feat = featurize(query_proj, previous[0], featurizer[0])
    key_feat = featurize(key_proj, previous[1], featurizer[1])
    value_feat = featurize(value_proj, previous[2], featurizer[2])
    upstream_f = upstream.astype(jnp.float32)
    grad_qfeat = upstream_f * saved_conv.astype(jnp.float32)
    grad_conv = (upstream_f * query_feat).astype(jnp.bfloat16)
    empty = jnp.zeros((block_rows, channels), jnp.float32)
    piece = lax.all_gather(grad_conv, "ctx", axis=0, tiled=True)
    piece_start = jnp.int32(0)
    grad_mix = lax.cond(
        piece_start + piece.shape[0] > own_start,
        lambda: cross_terms(
            piece, piece_start, own_start, block_rows, filt_pad, front_pad, tile_rows
        ),
        lambda: empty,
    )
    grad_kfeat = grad_mix * value_feat
    grad_vfeat = grad_mix * key_feat
    following = shifted(
        (grad_qfeat[: TAPS - 1], grad_kfeat[: TAPS - 1], grad_vfeat[: TAPS - 1]), "ctx", -1
    )
    grad_query = spread(grad_qfeat, following[0], featurizer[0]).astype(jnp.bfloat16)
    grad_key = spread(grad_kfeat, following[1], featurizer[1]).astype(jnp.bfloat16)
    grad_value = spread(grad_vfeat, following[2], featurizer[2]).astype(jnp.bfloat16)
    return (grad_query, grad_key, grad_value)


def solution(mesh):
    return jax.shard_map(
        body,
        mesh=mesh,
        in_specs=(
            P("ctx", "tp"),
            P("ctx", "tp"),
            P("ctx", "tp"),
            P("ctx", "tp"),
            P(("ctx", "tp"), None),
            P("tp", None),
            P(None, None, "tp"),
        ),
        out_specs=(P("ctx", "tp"), P("ctx", "tp"), P("ctx", "tp")),
        check_vma=False,
    )
```

profile of v0, /device:TPU:1, one launch (start us, length us, event | category | flops | bytes accessed | tf_op | source)
XLA Modules:
  0.0 704.6 jit_solution(5903635782921676362)
XLA Ops:
  7.9 6.9 collective-permute-start.1
  16.5 4.6 all-to-all-start
  23.8 4.0 all-to-all-done
  30.7 5.2 collective-permute-start.2
  45.7 48.6 %all-gather.2.cloned.1.call-done = bf16[6144,512]{1,0:T(8,128)(2,1)} async-done(((bf16[384,512]{1,0:T(8,128)(2,1)}), bf16[6144,512]{1,0:T(8,128)(2,1)}) %all-gather.2.cloned.1.call-update) | async-done | bytes 6291472 | tf_op jit(solution)/shard_map/all_gather | solution.py:94
  94.4 589.0 %conditional.1 = (f32[384,512]{1,0:T(8,128)}) conditional(s32[]{:T(128)} %convert_element_type.43, () %tuple.355, (bf16[32,6144]{1,0:T(8,128)(2,1)}, s32[]{:T(128)}, bf16[6144,512]{1,0:T(8,128)(2,1)}) %tuple.356), branch_computations={%region_0.1_spmd, %region_1.2_spmd} | conditional | flops 2425290752 | bytes 657653696 | solution.py:96
  95.8 17.2 %tile.1 = bf16[32,128,6528]{2,1,0:T(8,128)(2,1)} broadcast(bf16[32,6528]{1,0:T(8,128)(2,1)S(1)} %concatenate.114), dimensions={0,2} | broadcast | bytes 53895168 | tf_op jit(solution)/shard_map/cond/branch_1_fun/tile | solution.py:37
  113.0 49.0 %copy.164 = bf16[4,8,128,6528]{3,1,2,0:T(8,128)(2,1)} copy(bf16[4,8,128,6528]{3,2,1,0:T(8,128)(2,1)} %bitcast.572) | data formatting | bytes 106954752 | tf_op jit(solution)/shard_map/cond
  162.0 35.7 %slice.1975 = bf16[32,835456]{1,0:T(8,128)(2,1)} slice(bf16[32,835584]{1,0:T(8,128)(2,1)} %bitcast.573), slice={[0:32], [0:835456]} | slice | bytes 106938368 | tf_op jit(solution)/shard_map/cond/branch_1_fun/slice | solution.py:38
  197.7 208.9 %reshape.2132 = bf16[32,128,6527]{2,1,0:T(8,128)(2,1)} reshape(bf16[32,835456]{1,0:T(8,128)(2,1)} %slice.1975) | data formatting | bytes 106938368 | tf_op jit(solution)/shard_map/cond/branch_1_fun/reshape | solution.py:38
  406.5 8.9 %copy.159 = bf16[6144,512]{0,1:T(8,128)(2,1)} copy(bf16[6144,512]{1,0:T(8,128)(2,1)} %get-tuple-element.998) | data formatting | bytes 12582912 | tf_op jit(solution)/shard_map
  416.6 2.3 fusion.97
  423.1 6.3 fusion.131
  430.9 3.4 fusion.95
  434.3 6.4 fusion.132
  442.1 3.4 fusion.49
  447.0 3.4 fusion.47
  451.9 3.4 fusion.45
  456.8 3.4 fusion.43
  461.6 3.4 fusion.41
  466.5 3.4 fusion.39
  471.8 3.4 fusion.37
  476.7 3.4 fusion.35
  481.5 3.4 fusion.33
  486.4 3.4 fusion.31
  491.3 3.4 fusion.93
  496.2 3.4 fusion.29
  501.0 3.4 fusion.27
  505.9 3.4 fusion.25
  510.8 3.4 fusion.23
  515.6 3.4 fusion.21
  520.7 3.4 fusion.19
  525.5 3.4 fusion.17
  530.4 3.4 fusion.15
  535.3 3.4 fusion.13
  540.2 3.4 fusion.11
  545.1 3.4 fusion.9
  549.9 3.4 fusion.7
  554.8 3.4 fusion.5
  559.7 3.5 fusion.75
  564.6 3.4 fusion.73
  569.7 3.4 fusion.71
  574.6 3.4 fusion.69
  579.4 3.4 fusion.67
  584.3 3.4 fusion.65
  589.2 3.4 fusion.63
  594.0 3.4 fusion.61
  598.9 3.4 fusion.59
  603.8 3.4 fusion.57
  608.7 3.4 fusion.55
  613.5 3.4 fusion.53
  618.8 3.4 fusion.51
  622.2 3.7 fusion.133
  627.4 3.4 fusion.91
  632.2 3.4 fusion.89
  637.1 3.4 fusion.87
  642.0 3.4 fusion.85
  646.9 3.4 fusion.83
  651.7 3.4 fusion.81
  656.6 3.4 fusion.79
  661.5 2.5 fusion.77
  664.0 12.7 %bitcast_add_fusion = f32[3,128,32,16]{1,3,2,0:T(8,128)S(1)} fusion(f32[3,128,32,16]{1,3,2,0:T(8,128)S(1)} %fusion.100, f32[32,128,3,16]{1,3,2,0:T(8,128)} %bitcast.600, f32[32,128,3,16]{1,3,2,0:T(8,128)} %bitcast.599, f32[32,128,3,16]{1,3,2,0:T(8,128)} %bitcast.598, f32[32,128,3,16]{1,3,2,0:T(8,128)} %bitcast.597, f32[32,128,3,16]{1,3,2,0:T(8,128)} %bitcast.596, ...), kind=kLoop, calls=%fused_computation.104 | loop fusion | flops 9043968 | bytes 37748736 | tf_op jit(solution)/shard_map/cond/branch_1_fun/add | solution.py:66
  687.4 2.8 fusion.115
  693.1 3.5 collective-permute-done.3
  (159 shorter events, 106.7 us)
Async XLA Ops:
  7.9 14.8 %collective-permute-start.1 = (bf16[2,512]{1,0:T(2,128)(2,1)S(1)}, bf16[2,512]{1,0:T(2,128)(2,1)S(1)}, u32[]{:S(2)}, u32[]{:S(2)}) collective-permute-start(bf16[2,512]{1,0:T(2,128)(2,1)S(1)} %slice.1952), channel_id=1, source_target_pairs={{0,8},{8,16},{16,24},{24,32},{32,40},{40,48},{48,56},{56,64},{64,7... | collective-permute-start | bytes 6152 | tf_op jit(solution)/shard_map/ppermute | solution.py:13
  16.5 11.3 %all-to-all-start = ((bf16[48,8,512]{2,0,1:T(8,128)(2,1)}), bf16[48,8,512]{2,0,1:T(8,128)(2,1)S(1)}, u32[]{:S(2)}, u32[]{:S(2)}) async-start(bf16[48,8,512]{2,0,1:T(8,128)(2,1)} %bitcast.571), calls=%async_computation | async-start | bytes 786432 | tf_op jit(solution)/shard_map/all_to_all | solution.py:77
  21.2 73.2 %all-gather.2.cloned.1.call-start = ((), (), s32[]{:S(2)}) async-start(), calls=%async_computation.1 | async-start | bytes 6684672 | tf_op jit(solution)/shard_map/all_gather | solution.py:94
  22.7 71.7 %copy-start.3 = (f32[1,1,512]{2,1,0:T(1,128)}, f32[1,1,512]{2,1,0:T(1,128)S(1)}, u32[]{:S(2)}) copy-start(f32[1,1,512]{2,1,0:T(1,128)S(1)} %get-tuple-element.1060) | copy-start | bytes 6148
  22.7 71.7 %copy-start.4 = (f32[1,1,512]{2,1,0:T(1,128)}, f32[1,1,512]{2,1,0:T(1,128)S(1)}, u32[]{:S(2)}) copy-start(f32[1,1,512]{2,1,0:T(1,128)S(1)} %get-tuple-element.1061) | copy-start | bytes 6148
  22.7 71.7 %copy-start.5 = (f32[1,1,512]{2,1,0:T(1,128)}, f32[1,1,512]{2,1,0:T(1,128)S(1)}, u32[]{:S(2)}) copy-start(f32[1,1,512]{2,1,0:T(1,128)S(1)} %get-tuple-element.1062) | copy-start | bytes 6148
  30.0 64.4 %copy-start.2 = (f32[384,512]{1,0:T(8,128)}, f32[384,512]{1,0:T(8,128)S(1)}, u32[]{:S(2)}) copy-start(f32[384,512]{1,0:T(8,128)S(1)} %get-tuple-element.1055) | copy-start | bytes 2359300
  30.7 8.0 %collective-permute-start.2 = (bf16[2,512]{1,0:T(2,128)(2,1)S(1)}, bf16[2,512]{1,0:T(2,128)(2,1)S(1)}, u32[]{:S(2)}, u32[]{:S(2)}) collective-permute-start(bf16[2,512]{1,0:T(2,128)(2,1)S(1)} %slice.1957), channel_id=1, source_target_pairs={{0,8},{8,16},{16,24},{24,32},{32,40},{40,48},{48,56},{56,64},{64,7... | collective-permute-start | bytes 6152 | tf_op jit(solution)/shard_map/ppermute | solution.py:13
  36.7 4.2 collective-permute-start.4
  43.5 643.9 %collective-permute-start = (f32[2,512]{1,0:T(2,128)}, f32[2,512]{1,0:T(2,128)}, u32[]{:S(2)}, u32[]{:S(2)}) collective-permute-start(f32[2,512]{1,0:T(2,128)} %slice.2078), channel_id=1, source_target_pairs={{8,0},{16,8},{24,16},{32,24},{40,32},{48,40},{56,48},{64,56},{72,6... | collective-permute-start | bytes 12296 | tf_op jit(solution)/shard_map/ppermute | solution.py:13
  94.4 589.1 %copy-start = (f32[386,512]{1,0:T(8,128)S(1)}, f32[386,512]{1,0:T(8,128)}, u32[]{:S(2)}) copy-start(f32[386,512]{1,0:T(8,128)} %maximum_convert_fusion.1) | copy-start | bytes 2371588
  94.4 589.1 %copy-start.1 = (f32[386,512]{1,0:T(8,128)S(1)}, f32[386,512]{1,0:T(8,128)}, u32[]{:S(2)}) copy-start(f32[386,512]{1,0:T(8,128)} %maximum_convert_fusion.2) | copy-start | bytes 2371588
  94.4 589.1 %copy-start.6 = (f32[1,1,512]{2,1,0:T(1,128)S(1)}, f32[1,1,512]{2,1,0:T(1,128)}, u32[]{:S(2)}) copy-start(f32[1,1,512]{2,1,0:T(1,128)} %get-tuple-element.1056) | copy-start | bytes 6148
  94.4 589.1 %copy-start.7 = (f32[1,1,512]{2,1,0:T(1,128)S(1)}, f32[1,1,512]{2,1,0:T(1,128)}, u32[]{:S(2)}) copy-start(f32[1,1,512]{2,1,0:T(1,128)} %get-tuple-element.1063) | copy-start | bytes 6148
  94.4 589.1 %copy-start.8 = (f32[1,1,512]{2,1,0:T(1,128)S(1)}, f32[1,1,512]{2,1,0:T(1,128)}, u32[]{:S(2)}) copy-start(f32[1,1,512]{2,1,0:T(1,128)} %get-tuple-element.1064) | copy-start | bytes 6148
  94.4 589.1 %copy-start.9 = (f32[1,1,512]{2,1,0:T(1,128)S(1)}, f32[1,1,512]{2,1,0:T(1,128)}, u32[]{:S(2)}) copy-start(f32[1,1,512]{2,1,0:T(1,128)} %get-tuple-element.1057) | copy-start | bytes 6148
  94.4 589.1 %copy-start.10 = (f32[1,1,512]{2,1,0:T(1,128)S(1)}, f32[1,1,512]{2,1,0:T(1,128)}, u32[]{:S(2)}) copy-start(f32[1,1,512]{2,1,0:T(1,128)} %get-tuple-element.1058) | copy-start | bytes 6148
  94.4 589.1 %copy-start.11 = (f32[1,1,512]{2,1,0:T(1,128)S(1)}, f32[1,1,512]{2,1,0:T(1,128)}, u32[]{:S(2)}) copy-start(f32[1,1,512]{2,1,0:T(1,128)} %get-tuple-element.1059) | copy-start | bytes 6148
  685.2 6.9 collective-permute-start.5
  690.2 6.4 collective-permute-start.3
Sparse Core Ops, SparseCore 0:
  30.1 64.1 all-gather.1
where the time goes:
time: 712 us; the launch traced here: 705 us
  local copies, waits for them, and re-layouts  416 us (58%)
  matrix products  165 us (23%)
  waiting for transfers between devices  56.2 us (8%)
  other arithmetic  26.8 us (4%)
  starting transfers between devices  25.2 us (4%)
  between operations  14.4 us (2%)
    reshape x1, local copies, waits for them, and re-layouts, toeplitz_tiles(): tiled[:, :tile_rows * (width_k + tile_rows - 1)]  209 us
    cond x48, matrix products  161 us
    slice x101, local copies, waits for them, and re-layouts, cross_terms(): pieces[lowest + offset:highest + offset]  87 us
    cond x2, local copies, waits for them, and re-layouts  49.1 us
    all_gather x1, waiting for transfers between devices, body(): piece = lax.all_gather(grad_conv, 'ctx', axis=0, tiled=True)  48.6 us
    slice x1, local copies, waits for them, and re-layouts, toeplitz_tiles(): tiled[:, :tile_rows * (width_k + tile_rows - 1)]  35.7 us
    ppermute x6, starting transfers between devices, shifted(): return lax.ppermute(array, axis, pairs)  20.5 us
    another operation x1, local copies, waits for them, and re-layouts, toeplitz_tiles(): tiled = jnp.tile(padded, (1, tile_rows))  17.2 us
  transfers between devices with their start and end apart: 8, of which 3 were waited for; matrix products, arithmetic and copies ran while one was open for 86% of the time, Pallas kernels for 0%

commit v1 on v0

v1 whole, which is shorter than its diff:
```python
import jax
import jax.numpy as jnp
from jax import lax
from jax.experimental import pallas as pl
from jax.experimental.pallas import tpu as pltpu
from jax.sharding import PartitionSpec as P

GSIZE = 16
TAPS = 3
LANE = 128
HALO = 8
BLOCK = 256
MESH = pl.DeviceIdType.MESH


def kernel(
    n_ctx,
    n_tp,
    q_hbm,
    k_hbm,
    v_hbm,
    sc_hbm,
    go_hbm,
    filt_hbm,
    taps,
    oq_hbm,
    ok_hbm,
    ov_hbm,
    q_v,
    k_v,
    v_v,
    sc_v,
    go_v,
    filt_v,
    prev_v,
    next_v,
    join,
    qfeat,
    kfeat,
    vfeat,
    gq,
    toep,
    gct,
    land,
    xrows,
    acc,
    back,
    mix,
    prod,
    oq_v,
    ok_v,
    ov_v,
    local_sem,
    tp_send,
    tp_recv,
    halo_send,
    halo_recv,
    fwd_send,
    fwd_recv,
    bwd_send,
    bwd_recv,
    out_sem,
):
    me = lax.axis_index("ctx")
    mytp = lax.axis_index("tp")
    rows, channels = q_v.shape
    own_rows = go_hbm.shape[0]
    tokens = filt_v.shape[1]
    half_ch = channels // 2
    blocks = channels // LANE
    tiles = rows // LANE
    up = lax.rem(me + 1, n_ctx)
    down = lax.rem(me + n_ctx - 1, n_ctx)

    loads = []
    for index, (src, dst) in enumerate(
        ((q_hbm, q_v), (filt_hbm, filt_v), (k_hbm, k_v), (v_hbm, v_v), (sc_hbm, sc_v))
    ):
        copy = pltpu.make_async_copy(src, dst, local_sem.at[index])
        copy.start()
        loads.append(copy)
    own_go = pltpu.make_async_copy(
        go_hbm.at[:, pl.ds(pl.multiple_of(mytp * channels, channels), channels)],
        go_v.at[pl.ds(pl.multiple_of(mytp * own_rows, own_rows), own_rows), :],
        local_sem.at[5],
    )
    own_go.start()

    barrier = pltpu.get_barrier_semaphore()
    for step in range(1, n_tp):
        pl.semaphore_signal(
            barrier, inc=1, device_id={"tp": lax.rem(mytp + step, n_tp)}, device_id_type=MESH
        )
    for step in range(1, n_ctx):
        pl.semaphore_signal(
            barrier, inc=1, device_id={"ctx": lax.rem(me + step, n_ctx)}, device_id_type=MESH
        )
    pl.semaphore_wait(barrier, n_tp + n_ctx - 2)

    tp_copies = []
    for step in range(1, n_tp):
        peer = lax.rem(mytp + step, n_tp)
        copy = pltpu.make_async_remote_copy(
            src_ref=go_hbm.at[:, pl.ds(pl.multiple_of(peer * channels, channels), channels)],
            dst_ref=go_v.at[pl.ds(pl.multiple_of(mytp * own_rows, own_rows), own_rows), :],
            send_sem=tp_send.at[step],
            recv_sem=tp_recv.at[step],
            device_id={"tp": peer},
            device_id_type=MESH,
        )
        copy.start()
        tp_copies.append(copy)

    halo_copies = []
    for index, src in enumerate((q_hbm, k_hbm, v_hbm)):
        copy = pltpu.make_async_remote_copy(
            src_ref=src.at[pl.ds(rows - HALO, HALO), :],
            dst_ref=prev_v.at[index],
            send_sem=halo_send.at[index],
            recv_sem=halo_recv.at[index],
            device_id={"ctx": up},
            device_id_type=MESH,
        )
        copy.start()
        halo_copies.append(copy)
    for index, src in enumerate((k_hbm, v_hbm)):
        copy = pltpu.make_async_remote_copy(
            src_ref=src.at[pl.ds(0, HALO), :],
            dst_ref=next_v.at[index],
            send_sem=halo_send.at[3 + index],
            recv_sem=halo_recv.at[3 + index],
            device_id={"ctx": down},
            device_id_type=MESH,
        )
        copy.start()
        halo_copies.append(copy)

    loads[1].wait()
    n_groups = filt_v.shape[0]
    flip = (
        lax.broadcasted_iota(jnp.int32, (LANE, LANE), 0)
        + lax.broadcasted_iota(jnp.int32, (LANE, LANE), 1)
        == LANE - 1
    ).astype(jnp.float32).astype(jnp.bfloat16)
    lag_tiles = tokens // LANE
    for half in range(2):
        pick = (
            lax.broadcasted_iota(jnp.int32, (16, n_groups), 1) == me + half * n_ctx
        ).astype(jnp.float32).astype(jnp.bfloat16)
        line = jnp.dot(pick, filt_v[...], preferred_element_type=jnp.float32)
        line = line.astype(jnp.bfloat16)
        stack = jnp.concatenate(
            [line[:, LANE * t : LANE * (t + 1)] for t in range(lag_tiles - 1, -1, -1)], axis=0
        )
        turned = jnp.dot(stack, flip, preferred_element_type=jnp.float32)
        turned = jnp.concatenate(
            [turned[16 * t : 16 * t + 8] for t in range(lag_tiles)]
            + [jnp.zeros((8, 2 * LANE), jnp.float32)],
            axis=1,
        )
        base = pltpu.roll(turned, 1, 1, stride=1, stride_axis=0)
        for part in range(LANE // 16):
            toep[half, 16 * part : 16 * (part + 1), :] = jnp.concatenate(
                [
                    base if part == 0 else pltpu.roll(base, 16 * part, 1),
                    pltpu.roll(base, 16 * part + 8, 1),
                ],
                axis=0,
            ).astype(jnp.bfloat16)

    def columns(block):
        return slice(LANE * block, LANE * (block + 1))

    def feature(stream, current, block, following, count):
        before = prev_v[stream, :, columns(block)].astype(jnp.float32)
        join[0:HALO] = jnp.where(me == 0, 0.0, before)
        join[HALO : HALO + rows] = current[:, columns(block)].astype(jnp.float32)
        if following is not None:
            join[HALO + rows : 2 * HALO + rows] = next_v[following, :, columns(block)].astype(
                jnp.float32
            )
        total = taps[stream, 0:1, columns(block)] * join[HALO : HALO + count]
        for offset in range(1, TAPS):
            total = total + taps[stream, offset : offset + 1, columns(block)] * (
                join[HALO - offset : HALO - offset + count]
            )
        return total

    loads[0].wait()
    halo_copies[0].wait()
    for block in range(blocks):
        qfeat[block] = feature(0, q_v, block, None, rows)

    own_go.wait()
    for copy in tp_copies:
        copy.wait()
    fwd_copies = [[], []]
    for half in range(2):
        for block in range(half * blocks // 2, (half + 1) * blocks // 2):
            conv = go_v[:, columns(block)].astype(jnp.float32) * qfeat[block]
            gct[columns(block), :] = conv.T.astype(jnp.bfloat16)
        for step in range(1, n_ctx):
            peer = lax.rem(me + step, n_ctx)
            copy = pltpu.make_async_remote_copy(
                src_ref=gct.at[pl.ds(pl.multiple_of(half * half_ch + peer * GSIZE, GSIZE), GSIZE), :],
                dst_ref=land.at[half, me],
                send_sem=fwd_send.at[half, step],
                recv_sem=fwd_recv.at[half, step],
                device_id={"ctx": peer},
                device_id_type=MESH,
            )
            copy.start()
            fwd_copies[half].append(copy)
        land[half, me] = gct[
            pl.ds(pl.multiple_of(half * half_ch + me * GSIZE, GSIZE), GSIZE), :
        ]

    loads[4].wait()
    for block in range(blocks):
        gq[block, 0:rows] = go_v[:, columns(block)].astype(jnp.float32) * sc_v[
            :, columns(block)
        ].astype(jnp.float32)
    gq_copy = pltpu.make_async_remote_copy(
        src_ref=gq.at[:, pl.ds(0, HALO), :],
        dst_ref=gq.at[:, pl.ds(rows, HALO), :],
        send_sem=halo_send.at[5],
        recv_sem=halo_recv.at[5],
        device_id={"ctx": down},
        device_id_type=MESH,
    )
    gq_copy.start()
    loads[2].wait()
    loads[3].wait()
    for copy in halo_copies[1:]:
        copy.wait()
    for block in range(blocks):
        kfeat[block] = feature(1, k_v, block, 0, rows + HALO)
        vfeat[block] = feature(2, v_v, block, 1, rows + HALO)

    bwd_copies = [[], []]
    row_blocks = tokens // BLOCK
    for half in range(2):
        xrows[row_blocks * GSIZE :] = jnp.zeros(
            (xrows.shape[0] - row_blocks * GSIZE, BLOCK), jnp.bfloat16
        )
        for copy in fwd_copies[half]:
            copy.wait()
        for source in range(n_ctx):
            for tile in range(tiles):
                place, side = divmod(source * tiles + tile, 2)
                xrows[GSIZE * place : GSIZE * (place + 1), columns(side)] = land[
                    half, source, :, columns(tile)
                ]
        for part in range(3):
            amount = row_blocks * GSIZE - part * LANE
            left = jnp.concatenate(
                [xrows[GSIZE * d : GSIZE * d + amount, :] for d in range(8 * part, 8 * part + 8)],
                axis=1,
            )
            right = jnp.concatenate(
                [
                    toep[half, :, LANE * (lag_tiles - e) : LANE * (lag_tiles - e + 2)]
                    for e in range(16 * part, 16 * part + 16)
                ],
                axis=0,
            )
            product = jnp.dot(left, right, preferred_element_type=jnp.float32)
            if part == 0:
                acc[...] = product
            else:
                acc[0:amount] += product
        for target in range(n_ctx):
            for tile in range(tiles + 1):
                place, side = divmod(target * tiles + tile, 2)
                if place < row_blocks:
                    value = acc[GSIZE * place : GSIZE * (place + 1), columns(side)]
                else:
                    value = jnp.zeros((GSIZE, LANE), jnp.float32)
                back[half, target, :, columns(tile)] = value.astype(jnp.bfloat16)
        spot = pl.ds(pl.multiple_of(half * half_ch + me * GSIZE, GSIZE), GSIZE)
        for step in range(1, n_ctx):
            peer = lax.rem(me + step, n_ctx)
            copy = pltpu.make_async_remote_copy(
                src_ref=back.at[half, peer],
                dst_ref=mix.at[spot, :],
                send_sem=bwd_send.at[half, step],
                recv_sem=bwd_recv.at[half, step],
                device_id={"ctx": peer},
                device_id_type=MESH,
            )
            copy.start()
            bwd_copies[half].append(copy)
        mix[spot, :] = back[half, me]

    def spread(stream, load, block):
        total = taps[stream, 0:1, columns(block)] * load(0)
        for offset in range(1, TAPS):
            total = total + taps[stream, offset : offset + 1, columns(block)] * load(offset)
        return total.astype(jnp.bfloat16)

    gq_copy.wait()
    outs = []
    for block in range(blocks):
        gq[block, rows : rows + HALO] = jnp.where(
            me == n_ctx - 1, 0.0, gq[block, rows : rows + HALO]
        )
        oq_v[:, columns(block)] = spread(
            0, lambda offset: gq[block, offset : offset + rows], block
        )
    copy = pltpu.make_async_copy(oq_v, oq_hbm, out_sem.at[0])
    copy.start()
    outs.append(copy)

    for half in range(2):
        for copy in bwd_copies[half]:
            copy.wait()
        for block in range(half * blocks // 2, (half + 1) * blocks // 2):
            here = mix[columns(block), 0:rows].astype(jnp.float32).T
            there = mix[columns(block), rows : rows + LANE].astype(jnp.float32).T
            whole = jnp.concatenate([here, there[0:HALO]], axis=0)
            prod[0] = whole * vfeat[block]
            prod[1] = whole * kfeat[block]
            ok_v[:, columns(block)] = spread(
                1, lambda offset: prod[0, offset : offset + rows], block
            )
            ov_v[:, columns(block)] = spread(
                2, lambda offset: prod[1, offset : offset + rows], block
            )
        part = pl.ds(half * half_ch, half_ch)
        for index, (src, dst) in enumerate(((ok_v, ok_hbm), (ov_v, ov_hbm))):
            copy = pltpu.make_async_copy(
                src.at[:, part], dst.at[:, part], out_sem.at[1 + 2 * half + index]
            )
            copy.start()
            outs.append(copy)
    for copy in outs:
        copy.wait()


def body(n_ctx, n_tp, query_proj, key_proj, value_proj, saved_conv, grad_out, filters, featurizer):
    rows, channels = query_proj.shape
    tokens = filters.shape[1]
    blocks = channels // LANE
    bf16, f32 = jnp.bfloat16, jnp.float32
    dma = pltpu.SemaphoreType.DMA
    hbm = pl.BlockSpec(memory_space=pl.ANY)
    stream = pltpu.VMEM((rows, channels), bf16)
    conv_rows = tokens // BLOCK * GSIZE
    run = pl.pallas_call(
        lambda *refs: kernel(n_ctx, n_tp, *refs),
        out_shape=[jax.ShapeDtypeStruct((rows, channels), bf16)] * 3,
        in_specs=[hbm] * 6 + [pl.BlockSpec(memory_space=pltpu.VMEM)],
        out_specs=[hbm] * 3,
        scratch_shapes=[
            stream,
            stream,
            stream,
            stream,
            stream,
            pltpu.VMEM(filters.shape, bf16),
            pltpu.VMEM((3, HALO, channels), bf16),
            pltpu.VMEM((2, HALO, channels), bf16),
            pltpu.VMEM((rows + 2 * HALO, LANE), f32),
            pltpu.VMEM((blocks, rows, LANE), f32),
            pltpu.VMEM((blocks, rows + HALO, LANE), f32),
            pltpu.VMEM((blocks, rows + HALO, LANE), f32),
            pltpu.VMEM((blocks, rows + HALO, LANE), f32),
            pltpu.VMEM((2, LANE, tokens + 2 * LANE), bf16),
            pltpu.VMEM((channels, rows), bf16),
            pltpu.VMEM((2, n_ctx, GSIZE, rows), bf16),
            pltpu.VMEM((conv_rows + LANE, BLOCK), bf16),
            pltpu.VMEM((conv_rows, BLOCK), f32),
            pltpu.VMEM((2, n_ctx, GSIZE, rows + LANE), bf16),
            pltpu.VMEM((channels, rows + LANE), bf16),
            pltpu.VMEM((2, rows + HALO, LANE), f32),
            stream,
            stream,
            stream,
            dma((6,)),
            dma((n_tp,)),
            dma((n_tp,)),
            dma((6,)),
            dma((6,)),
            dma((2, n_ctx)),
            dma((2, n_ctx)),
            dma((2, n_ctx)),
            dma((2, n_ctx)),
            dma((5,)),
        ],
        compiler_params=pltpu.CompilerParams(collective_id=0, has_side_effects=True),
    )
    return tuple(
        run(query_proj, key_proj, value_proj, saved_conv, grad_out, filters, featurizer)
    )


def solution(mesh):
    n_ctx, n_tp = mesh.shape["ctx"], mesh.shape["tp"]
    return jax.shard_map(
        lambda *args: body(n_ctx, n_tp, *args),
        mesh=mesh,
        in_specs=(
            P("ctx", "tp"),
            P("ctx", "tp"),
            P("ctx", "tp"),
            P("ctx", "tp"),
            P(("ctx", "tp"), None),
            P("tp", None),
            P(None, None, "tp"),
        ),
        out_specs=(P("ctx", "tp"), P("ctx", "tp"), P("ctx", "tp")),
        check_vma=False,
    )
```

time: 712 us -> 40.6 us (0.06)
  local copies, waits for them, and re-layouts: 416 us -> 3.7 us
  matrix products: 165 us -> 0 us
  waiting for transfers between devices: 56.2 us -> 0 us
  Pallas kernels: 0 us -> 36 us
  other arithmetic: 26.8 us -> 0 us
  starting transfers between devices: 25.2 us -> 0 us
  between operations: 14.4 us -> 0.65 us
    reshape x1 -> x0, local copies, waits for them, and re-layouts: 209 us -> none  [toeplitz_tiles(): tiled[:, :tile_rows * (width_k + tile_rows - 1)]]
    cond x48 -> x0, matrix products: 161 us -> none
    slice x109 -> x0, local copies, waits for them, and re-layouts: 127 us -> none  [the longest x101 87 us: cross_terms(): pieces[lowest + offset:highest + offset]]
    cond x3 -> x0, local copies, waits for them, and re-layouts: 50.2 us -> none
    all_gather x1 -> x0, waiting for transfers between devices: 48.6 us -> none  [body(): piece = lax.all_gather(grad_conv, 'ctx', axis=0, tiled=True)]
    pallas_call x0 -> x1, Pallas kernels: none -> 36 us  [body(): run(query_proj, key_proj, value_proj, saved_conv, grad_out, filters, feat...]
    another operation x2 -> x0, local copies, waits for them, and re-layouts: 26.1 us -> none  [the longest x1 17.2 us: toeplitz_tiles(): tiled = jnp.tile(padded, (1, tile_rows))]
    ppermute x6 -> x0, starting transfers between devices: 20.5 us -> none  [shifted(): return lax.ppermute(array, axis, pairs)]
  transfers between devices with their start and end apart: 8 -> 0, of which waited for: 3 -> 0; matrix products, arithmetic and copies ran while one was open for 86% -> 0% of each run, Pallas kernels for 0% -> 0%
where the time goes in v1:
time: 40.6 us; the launch traced here: 40.3 us
  Pallas kernels  36 us (89%)
  local copies, waits for them, and re-layouts  3.7 us (9%)
  between operations  0.65 us (2%)
    pallas_call x1, Pallas kernels, body(): run(query_proj, key_proj, value_proj, saved_conv, grad_out, filters, feat...  36 us
    unnamed x7, local copies, waits for them, and re-layouts  3.7 us

profile of v1, /device:TPU:1, one launch (start us, length us, event | category | flops | bytes accessed | tf_op | source)
XLA Modules:
  0.0 40.3 jit_solution(12457741674930744276)
XLA Ops:
  0.6 36.0 %shard_map.94 = (bf16[384,512]{1,0:T(8,128)(2,1)}, bf16[384,512]{1,0:T(8,128)(2,1)}, bf16[384,512]{1,0:T(8,128)(2,1)}) custom-call(bf16[384,512]{1,0:T(8,128)(2,1)} %refs_0_.1, bf16[384,512]{1,0:T(8,128)(2,1)} %refs_1_.1, bf16[384,512]{1,0:T(8,128)(2,1)} %refs_2_.1, bf16[384,512]{1,0:T(8,128)(2,1)} %refs_3_.1, bf16[48,4096]{1,0:T(8,128)(2,1)} %refs_4_.1, ...), custom_call_target="tpu_custom_call" | custom-call | tf_op jit(solution)/shard_map/pallas_call | solution.py:393
  36.6 0.0 copy-start.1
  36.6 1.8 %copy.13 = bf16[384,512]{1,0:T(8,128)(2,1)} copy(bf16[384,512]{1,0:T(8,128)(2,1)} %get-tuple-element.6) | data formatting | bytes 786432
  38.4 0.0 copy-done.1
  38.4 0.0 copy-start
  38.4 0.7 %copy.14 = bf16[384,512]{1,0:T(8,128)(2,1)} copy(bf16[384,512]{1,0:T(8,128)(2,1)S(1)} %copy-done.1) | data formatting | bytes 786432
  39.2 0.4 copy-done
  39.6 0.7 %copy.15 = bf16[384,512]{1,0:T(8,128)(2,1)} copy(bf16[384,512]{1,0:T(8,128)(2,1)S(1)} %copy-done) | data formatting | bytes 786432
Async XLA Ops:
  36.6 1.8 %copy-start.1 = (bf16[384,512]{1,0:T(8,128)(2,1)S(1)}, bf16[384,512]{1,0:T(8,128)(2,1)}, u32[]{:S(2)}) copy-start(bf16[384,512]{1,0:T(8,128)(2,1)} %get-tuple-element.7) | copy-start | bytes 1179652
  38.4 1.1 %copy-start = (bf16[384,512]{1,0:T(8,128)(2,1)S(1)}, bf16[384,512]{1,0:T(8,128)(2,1)}, u32[]{:S(2)}) copy-start(bf16[384,512]{1,0:T(8,128)(2,1)} %get-tuple-element.8) | copy-start | bytes 1179652

commit v2 on v1

--- a/solution.py
+++ b/solution.py
@@ -22,10 +22,14 @@
     sc_hbm,
     go_hbm,
     filt_hbm,
+    taps_hbm,
     taps,
-    oq_hbm,
-    ok_hbm,
-    ov_hbm,
+    oq_v,
+    ok_v,
+    ov_v,
+    mix,
+    kfeat,
+    vfeat,
     q_v,
     k_v,
     v_v,
@@ -36,8 +40,6 @@
     next_v,
     join,
     qfeat,
-    kfeat,
-    vfeat,
     gq,
     toep,
     gct,
@@ -45,11 +47,7 @@
     xrows,
     acc,
     back,
-    mix,
     prod,
-    oq_v,
-    ok_v,
-    ov_v,
     local_sem,
     tp_send,
     tp_recv,
@@ -59,7 +57,6 @@
     fwd_recv,
     bwd_send,
     bwd_recv,
-    out_sem,
 ):
     me = lax.axis_index("ctx")
     mytp = lax.axis_index("tp")
@@ -74,7 +71,14 @@
 
     loads = []
     for index, (src, dst) in enumerate(
-        ((q_hbm, q_v), (filt_hbm, filt_v), (k_hbm, k_v), (v_hbm, v_v), (sc_hbm, sc_v))
+        (
+            (q_hbm, q_v),
+            (filt_hbm, filt_v),
+            (k_hbm, k_v),
+            (v_hbm, v_v),
+            (sc_hbm, sc_v),
+            (taps_hbm, taps),
+        )
     ):
         copy = pltpu.make_async_copy(src, dst, local_sem.at[index])
         copy.start()
@@ -82,7 +86,7 @@
     own_go = pltpu.make_async_copy(
         go_hbm.at[:, pl.ds(pl.multiple_of(mytp * channels, channels), channels)],
         go_v.at[pl.ds(pl.multiple_of(mytp * own_rows, own_rows), own_rows), :],
-        local_sem.at[5],
+        local_sem.at[6],
     )
     own_go.start()
 
@@ -97,19 +101,24 @@
         )
     pl.semaphore_wait(barrier, n_tp + n_ctx - 2)
 
-    tp_copies = []
-    for step in range(1, n_tp):
-        peer = lax.rem(mytp + step, n_tp)
-        copy = pltpu.make_async_remote_copy(
-            src_ref=go_hbm.at[:, pl.ds(pl.multiple_of(peer * channels, channels), channels)],
-            dst_ref=go_v.at[pl.ds(pl.multiple_of(mytp * own_rows, own_rows), own_rows), :],
-            send_sem=tp_send.at[step],
-            recv_sem=tp_recv.at[step],
-            device_id={"tp": peer},
-            device_id_type=MESH,
-        )
-        copy.start()
-        tp_copies.append(copy)
+    tp_copies = [[], []]
+    for half in range(2):
+        for step in range(1, n_tp):
+            peer = lax.rem(mytp + step, n_tp)
+            source = pl.multiple_of(peer * channels + half * half_ch, half_ch)
+            copy = pltpu.make_async_remote_copy(
+                src_ref=go_hbm.at[:, pl.ds(source, half_ch)],
+                dst_ref=go_v.at[
+                    pl.ds(pl.multiple_of(mytp * own_rows, own_rows), own_rows),
+                    pl.ds(half * half_ch, half_ch),
+                ],
+                send_sem=tp_send.at[half, step],
+                recv_sem=tp_recv.at[half, step],
+                device_id={"tp": peer},
+                device_id_type=MESH,
+            )
+            copy.start()
+            tp_copies[half].append(copy)
 
     halo_copies = []
     for index, src in enumerate((q_hbm, k_hbm, v_hbm)):
@@ -187,15 +196,16 @@
         return total
 
     loads[0].wait()
+    loads[5].wait()
     halo_copies[0].wait()
     for block in range(blocks):
         qfeat[block] = feature(0, q_v, block, None, rows)
 
     own_go.wait()
-    for copy in tp_copies:
-        copy.wait()
     fwd_copies = [[], []]
     for half in range(2):
+        for copy in tp_copies[half]:
+            copy.wait()
         for block in range(half * blocks // 2, (half + 1) * blocks // 2):
             conv = go_v[:, columns(block)].astype(jnp.float32) * qfeat[block]
             gct[columns(block), :] = conv.T.astype(jnp.bfloat16)
@@ -292,48 +302,62 @@
             bwd_copies[half].append(copy)
         mix[spot, :] = back[half, me]
 
-    def spread(stream, load, block):
-        total = taps[stream, 0:1, columns(block)] * load(0)
-        for offset in range(1, TAPS):
-            total = total + taps[stream, offset : offset + 1, columns(block)] * load(offset)
-        return total.astype(jnp.bfloat16)
-
     gq_copy.wait()
-    outs = []
     for block in range(blocks):
         gq[block, rows : rows + HALO] = jnp.where(
             me == n_ctx - 1, 0.0, gq[block, rows : rows + HALO]
         )
-        oq_v[:, columns(block)] = spread(
-            0, lambda offset: gq[block, offset : offset + rows], block
-        )
-    copy = pltpu.make_async_copy(oq_v, oq_hbm, out_sem.at[0])
-    copy.start()
-    outs.append(copy)
-
-    for half in range(2):
-        for copy in bwd_copies[half]:
-            copy.wait()
-        for block in range(half * blocks // 2, (half + 1) * blocks // 2):
-            here = mix[columns(block), 0:rows].astype(jnp.float32).T
-            there = mix[columns(block), rows : rows + LANE].astype(jnp.float32).T
-            whole = jnp.concatenate([here, there[0:HALO]], axis=0)
-            prod[0] = whole * vfeat[block]
-            prod[1] = whole * kfeat[block]
-            ok_v[:, columns(block)] = spread(
-                1, lambda offset: prod[0, offset : offset + rows], block
-            )
-            ov_v[:, columns(block)] = spread(
-                2, lambda offset: prod[1, offset : offset + rows], block
-            )
-        part = pl.ds(half * half_ch, half_ch)
-        for index, (src, dst) in enumerate(((ok_v, ok_hbm), (ov_v, ov_hbm))):
+        oq_v[:, columns(block)] = spread(taps, 0, gq.at[block], block, rows)
+    for copy in bwd_copies[0]:
+        copy.wait()
+    for block in range(blocks // 2):
+        finish(taps, mix, kfeat, vfeat, prod, ok_v, ov_v, block, block, rows)
+    for copy in bwd_copies[1]:
+        copy.wait()
+
+
+def spread(taps, stream, source, block, rows):
+    where = slice(LANE * block, LANE * (block + 1))
+    total = taps[stream, 0:1, where] * source[0:rows]
+    for offset in range(1, TAPS):
+        total = total + taps[stream, offset : offset + 1, where] * source[offset : offset + rows]
+    return total.astype(jnp.bfloat16)
+
+
+def finish(taps, mix, kfeat, vfeat, prod, ok_v, ov_v, block, place, rows):
+    channel = slice(LANE * block, LANE * (block + 1))
+    target = slice(LANE * place, LANE * (place + 1))
+    here = mix[channel, 0:rows].astype(jnp.float32).T
+    there = mix[channel, rows : rows + LANE].astype(jnp.float32).T
+    whole = jnp.concatenate([here, there[0:HALO]], axis=0)
+    prod[0] = whole * vfeat[block]
+    prod[1] = whole * kfeat[block]
+    ok_v[:, target] = spread(taps, 1, prod.at[0], block, rows)
+    ov_v[:, target] = spread(taps, 2, prod.at[1], block, rows)
+
+
+def last_kernel(taps, oq_v, ok_v, ov_v, mix, kfeat, vfeat, oq, ok, ov, prod, ok_rest, ov_rest, sem):
+    rows, channels = oq_v.shape
+    half_ch = channels // 2
+    blocks = channels // LANE
+    copies = [
+        pltpu.make_async_copy(oq_v, oq, sem.at[0]),
+        pltpu.make_async_copy(ok_v, ok.at[:, pl.ds(0, half_ch)], sem.at[1]),
+        pltpu.make_async_copy(ov_v, ov.at[:, pl.ds(0, half_ch)], sem.at[2]),
+    ]
+    for copy in copies:
+        copy.start()
+    for index, block in enumerate(range(blocks // 2, blocks)):
+        finish(taps, mix, kfeat, vfeat, prod, ok_rest, ov_rest, block, index, rows)
+        for which, (src, dst) in enumerate(((ok_rest, ok), (ov_rest, ov))):
             copy = pltpu.make_async_copy(
-                src.at[:, part], dst.at[:, part], out_sem.at[1 + 2 * half + index]
+                src.at[:, pl.ds(LANE * index, LANE)],
+                dst.at[:, pl.ds(LANE * block, LANE)],
+                sem.at[3 + 2 * index + which],
             )
             copy.start()
-            outs.append(copy)
-    for copy in outs:
+            copies.append(copy)
+    for copy in copies:
         copy.wait()
 
 
@@ -346,11 +370,21 @@
     hbm = pl.BlockSpec(memory_space=pl.ANY)
     stream = pltpu.VMEM((rows, channels), bf16)
     conv_rows = tokens // BLOCK * GSIZE
-    run = pl.pallas_call(
+    vmem = pl.BlockSpec(memory_space=pltpu.VMEM)
+    between = [
+        pltpu.VMEM(featurizer.shape, f32),
+        pltpu.VMEM((rows, channels), bf16),
+        pltpu.VMEM((rows, channels // 2), bf16),
+        pltpu.VMEM((rows, channels // 2), bf16),
+        pltpu.VMEM((channels, rows + LANE), bf16),
+        pltpu.VMEM((blocks, rows + HALO, LANE), f32),
+        pltpu.VMEM((blocks, rows + HALO, LANE), f32),
+    ]
+    first = pl.pallas_call(
         lambda *refs: kernel(n_ctx, n_tp, *refs),
-        out_shape=[jax.ShapeDtypeStruct((rows, channels), bf16)] * 3,
-        in_specs=[hbm] * 6 + [pl.BlockSpec(memory_space=pltpu.VMEM)],
-        out_specs=[hbm] * 3,
+        out_shape=between,
+        in_specs=[hbm] * 7,
+        out_specs=[vmem] * 7,
         scratch_shapes=[
             stream,
             stream,
@@ -363,35 +397,42 @@
             pltpu.VMEM((rows + 2 * HALO, LANE), f32),
             pltpu.VMEM((blocks, rows, LANE), f32),
             pltpu.VMEM((blocks, rows + HALO, LANE), f32),
-            pltpu.VMEM((blocks, rows + HALO, LANE), f32),
-            pltpu.VMEM((blocks, rows + HALO, LANE), f32),
             pltpu.VMEM((2, LANE, tokens + 2 * LANE), bf16),
             pltpu.VMEM((channels, rows), bf16),
             pltpu.VMEM((2, n_ctx, GSIZE, rows), bf16),
             pltpu.VMEM((conv_rows + LANE, BLOCK), bf16),
             pltpu.VMEM((conv_rows, BLOCK), f32),
             pltpu.VMEM((2, n_ctx, GSIZE, rows + LANE), bf16),
-            pltpu.VMEM((channels, rows + LANE), bf16),
             pltpu.VMEM((2, rows + HALO, LANE), f32),
-            stream,
-            stream,
-            stream,
-            dma((6,)),
-            dma((n_tp,)),
-            dma((n_tp,)),
+            dma((7,)),
+            dma((2, n_tp)),
+            dma((2, n_tp)),
             dma((6,)),
             dma((6,)),
             dma((2, n_ctx)),
             dma((2, n_ctx)),
             dma((2, n_ctx)),
             dma((2, n_ctx)),
-            dma((5,)),
         ],
-        compiler_params=pltpu.CompilerParams(collective_id=0, has_side_effects=True),
+        compiler_params=pltpu.CompilerParams(
+            collective_id=0, has_side_effects=True, vmem_limit_bytes=64_000_000
+        ),
     )
-    return tuple(
-        run(query_proj, key_proj, value_proj, saved_conv, grad_out, filters, featurizer)
+    results = first(query_proj, key_proj, value_proj, saved_conv, grad_out, filters, featurizer)
+    last = pl.pallas_call(
+        last_kernel,
+        out_shape=[jax.ShapeDtypeStruct((rows, channels), bf16)] * 3,
+        in_specs=[vmem] * 7,
+        out_specs=[hbm] * 3,
+        scratch_shapes=[
+            pltpu.VMEM((2, rows + HALO, LANE), f32),
+            pltpu.VMEM((rows, channels // 2), bf16),
+            pltpu.VMEM((rows, channels // 2), bf16),
+            dma((3 + blocks,)),
+        ],
+        compiler_params=pltpu.CompilerParams(vmem_limit_bytes=16 << 20),
     )
+    return tuple(last(*results))
 
 
 def solution(mesh):

time: 40.6 us -> 35.5 us (0.87)
  local copies, waits for them, and re-layouts: 3.7 us -> 0 us
  Pallas kernels: 36 us -> 34.8 us
    unnamed x7 -> x0, local copies, waits for them, and re-layouts: 3.7 us -> none
    pallas_call x1 -> x2, Pallas kernels: 36 us -> 34.8 us  [the longest x1 33.7 us: body(): first(query_proj, key_proj, value_proj, saved_conv, grad_out, filters, fe...]
where the time goes in v2:
time: 35.5 us; the launch traced here: 35.4 us
  Pallas kernels  34.8 us (98%)
  between operations  0.64 us (2%)
    pallas_call x1, Pallas kernels, body(): first(query_proj, key_proj, value_proj, saved_conv, grad_out, filters, fe...  33.7 us
    pallas_call x1, Pallas kernels, body(): return tuple(last(*results))  1.11 us

profile of v2, /device:TPU:1, one launch (start us, length us, event | category | flops | bytes accessed | tf_op | source)
XLA Modules:
  0.0 35.4 jit_solution(2651584287130798598)
XLA Ops:
  0.6 33.7 %shard_map.94 = (f32[3,3,512]{2,1,0:T(4,128)S(1)}, bf16[384,512]{1,0:T(8,128)(2,1)S(1)}, bf16[384,256]{1,0:T(8,128)(2,1)S(1)}, bf16[384,256]{1,0:T(8,128)(2,1)S(...) custom-call(bf16[384,512]{1,0:T(8,128)(2,1)} %refs_0_.1, ...), custom_call_target="tpu_custom_call" | custom-call | tf_op jit(solution)/shard_map/pallas_call | solution.py:421
  34.3 1.1 %shard_map.95 = (bf16[384,512]{1,0:T(8,128)(2,1)}, bf16[384,512]{1,0:T(8,128)(2,1)}, bf16[384,512]{1,0:T(8,128)(2,1)}) custom-call(f32[3,3,512]{2,1,0:T(4,128)S(1)} %get-tuple-element.10.taps, bf16[384,512]{1,0:T(8,128)(2,1)S(1)} %get-tuple-element.11.oq_v, bf16[384,256]{1,0:T(8,128)(2,1)S(1)} %get-tuple-element.12.ok_v, ...), custom_call_target="tpu_custom_call" | custom-call | tf_op jit(solution)/shard_map/pallas_call | solution.py:435
